TPU v7x, 256 devices: a whole 4x4x8 slice. The times are simulated.
256 devices in a mesh: group: 16 (over z_lo, y), fsdp: 16 (over x, z_hi, core).
Axes of the slice: x: 4, y: 4, z: 8 (z_hi: 2, z_lo: 4; z = z_hi * 4 + z_lo), core: 2. Of those that a mesh axis runs over, the one named last changes fastest.
Arguments:
- frames: bfloat16 [16, 8192, 1280], P('group', 'fsdp'), may hold values from -6 to 6
- cotangent: bfloat16 [16, 8192, 1280], P('group', 'fsdp'), may hold values from -12 to 12
- mix_partner: int32 [16, 64], P('group', 'fsdp'), may hold values from 0 to 3
- lengths: int32 [16, 64], P('group', 'fsdp'), may hold values from 32 to 128, as said below
- inner_params: bfloat16 [16, 1280, 2, 2560], P('group', 'fsdp'), may hold values from -6 to 6
- first_moment: float32 [16, 1280, 2, 2560], P('group', 'fsdp'), may hold values from -6 to 6
- second_moment: float32 [16, 1280, 2, 2560], P('group', 'fsdp'), may hold values from 0.25 to 4
- outer_params: float32 [1280, 2, 2560], P('fsdp'), may hold values from -6 to 6
- momentum: float32 [1280, 2, 2560], P('fsdp'), may hold values from -3 to 3
Outputs:
- new_moment: float32 [16, 1280, 2, 2560], P('group', 'fsdp')
- new_outer: float32 [1280, 2, 2560], P('fsdp')
- new_momentum: float32 [1280, 2, 2560], P('fsdp')
Inputs may be any that keep to these rules, and one draw needn't show every extreme that they name: `lengths`: in every replica at least one utterance has all 128 frames.
All inputs are finite; a program needn't handle non-finite values.
Results may differ from a plain program's by a relative error of at most 0.004.
Values may be sent and summed in bfloat16 or wider, within the bound.
A program may use at most 128 MiB of HBM per device.

v0:
```python
import jax
import jax.numpy as jnp
from jax import lax
from jax.sharding import PartitionSpec as P

beta_one = 0.9
beta_two = 0.98
inner_rate = 0.08
decay_rate = 0.01
adam_eps = 1e-06
outer_rate = 0.7
nesterov_mu = 0.9
norm_eps = 1e-05
mix_weight = 0.5
inv_root_two = 0.7071067811865476
inv_root_tau = 0.3989422804014327
correction_one = 1.0 - beta_one**500.0
correction_two = 1.0 - beta_two**500.0


def gelu_parts(values):
    cumulative = 0.5 * (1.0 + jax.scipy.special.erf(values * inv_root_two))
    density = jnp.exp(-0.5 * values * values) * inv_root_tau
    return (values * cumulative, cumulative + values * density)


def normalize(mixed_rows):
    centre = jnp.mean(mixed_rows, axis=-1, keepdims=True)
    shifted = mixed_rows - centre
    spread = jnp.mean(shifted * shifted, axis=-1, keepdims=True)
    return (shifted * lax.rsqrt(spread + norm_eps)).astype(jnp.bfloat16)


def add_rows(left_rows, portion):
    return jnp.dot(left_rows, portion, preferred_element_type=jnp.float32)


def per_device(
    frames,
    cotangent,
    mix_partner,
    lengths,
    inner_params,
    first_moment,
    second_moment,
    outer_params,
    momentum,
):
    frame_rows = frames.shape[1]
    model_width = frames.shape[2]
    utt_count = mix_partner.shape[1]
    crop_frames = frame_rows // utt_count
    hidden_width = inner_params.shape[3]
    blocks = frames[0].reshape(utt_count, crop_frames, model_width).astype(jnp.float32)
    partner_rows = jnp.take(blocks, mix_partner[0], axis=0)
    mixed_rows = blocks + mix_weight * partner_rows
    normed = normalize(mixed_rows).reshape(frame_rows, model_width)
    offsets = lax.broadcasted_iota(jnp.int32, (utt_count, crop_frames), 1)
    keep_mask = (offsets < lengths[0][:, None]).reshape(frame_rows, 1).astype(jnp.bfloat16)
    masked_grad = cotangent[0] * keep_mask
    pre_sum = add_rows(normed, lax.all_gather(inner_params[0, :, 0, :], "fsdp", axis=0, tiled=True))
    back_sum = add_rows(
        masked_grad, lax.all_gather(inner_params[0, :, 1, :], "fsdp", axis=0, tiled=True)
    )
    pre_act = pre_sum * model_width ** (-0.5)
    back_grad = back_sum * hidden_width ** (-0.5)
    activation, derivative = gelu_parts(pre_act)
    activation = activation.astype(jnp.bfloat16)
    hidden_grad = (back_grad * derivative).astype(jnp.bfloat16)
    grad_in = lax.dot_general(
        normed, hidden_grad, (((0,), (0,)), ((), ())), preferred_element_type=jnp.float32
    ) * model_width ** (-0.5)
    grad_out = lax.dot_general(
        masked_grad, activation, (((0,), (0,)), ((), ())), preferred_element_type=jnp.float32
    ) * hidden_width ** (-0.5)
    gradients = lax.psum_scatter(
        jnp.stack((grad_in, grad_out), axis=1).astype(jnp.bfloat16),
        "fsdp",
        scatter_dimension=0,
        tiled=True,
    ).astype(jnp.float32)
    new_moment = beta_one * first_moment[0] + (1.0 - beta_one) * gradients
    new_second = beta_two * second_moment[0] + (1.0 - beta_two) * gradients * gradients
    update = new_moment / correction_one / (jnp.sqrt(new_second / correction_two) + adam_eps)
    current = inner_params[0].astype(jnp.float32)
    stepped = current - inner_rate * (update + decay_rate * current)
    pseudo = outer_params - stepped
    replica_count = lax.axis_size("group")
    totals = lax.psum(pseudo, "group")
    average = totals * (1.0 / replica_count)
    new_momentum = nesterov_mu * momentum + average
    new_outer = outer_params - outer_rate * (average + nesterov_mu * new_momentum)
    return (new_moment[None], new_outer, new_momentum)


def solution(mesh):
    in_specs = (
        P("group", "fsdp", None),
        P("group", "fsdp", None),
        P("group", "fsdp"),
        P("group", "fsdp"),
        P("group", "fsdp", None, None),
        P("group", "fsdp", None, None),
        P("group", "fsdp", None, None),
        P("fsdp", None, None),
        P("fsdp", None, None),
    )
    out_specs = (P("group", "fsdp", None, None), P("fsdp", None, None), P("fsdp", None, None))
    return jax.shard_map(
        per_device, mesh=mesh, in_specs=in_specs, out_specs=out_specs, check_vma=False
    )
```

profile of v0, /device:TPU:2, one launch (start us, length us, event | category | flops | bytes accessed | tf_op | source)
XLA Modules:
  0.0 577.6 jit_solution(5133253302970498098)
XLA Ops:
  7.2 0.0 copy-start
  7.2 0.0 all-gather.7.cloned.1.call-start
  7.2 2.9 fusion.36
  10.1 0.8 copy.50
  10.9 0.0 all-gather.7.cloned.1.call-update
  10.9 0.0 all-gather.5.cloned.1.call-start
  11.0 0.0 copy-start.7
  11.0 0.8 copy.51
  11.8 0.0 all-gather.5.cloned.1.call-update
  11.8 0.0 reduce-scatter.2.cloned.1.call-start
  11.9 0.0 copy-done
  11.9 1.7 convert.32
  13.6 0.0 copy-done.7
  13.6 0.0 copy-start.8
  13.6 2.5 gather_fusion
  16.1 0.0 copy-start.1
  16.1 0.1 broadcast_bitcast_fusion
  16.2 0.0 copy-done.8
  16.2 0.1 fusion.33
  16.2 2.0 fusion.28
  18.2 0.0 copy-done.1
  18.2 0.8 multiply_reduce_fusion
  19.0 1.7 fusion.16
  20.8 87.6 %all-gather.7.cloned.1.call-done = bf16[1,1280,1,2560]{3,1,2,0:T(8,128)(2,1)} async-done(((bf16[1,80,1,2560]{3,1,2,0:T(8,128)(2,1)}), bf16[1,1280,1,2560]{3,1,2,0:T(8,128)(2,1)}) %all-gather.7.cloned.1.call-update) | async-done | bytes 6553616 | tf_op jit(solution)/shard_map/all_gather | solution.py:61
  108.4 6.1 %fusion.4 = f32[512,2560]{1,0:T(8,128)S(1)} fusion(bf16[512,1280]{1,0:T(8,128)(2,1)} %fusion.16, bf16[1,1280,1,2560]{3,1,2,0:T(8,128)(2,1)} %all-gather.7.cloned.1.call-done), kind=kOutput, calls=%fused_computation.8 | convolution fusion | flops 3355443200 | bytes 13107200 | tf_op jit(solution)/shard_map/dot_general | solution.py:35
  114.4 0.0 copy-start.9
  114.4 2.3 copy-done.9
  116.7 0.0 copy-done.6
  116.7 5.8 %fusion.2 = bf16[1280,1,2560]{2,0,1:T(8,128)(2,1)} fusion(f32[512,2560]{1,0:T(8,128)S(1)} %fusion.4, bf16[1,512,1280]{2,1,0:T(8,128)(2,1)S(1)} %copy-done.6, bf16[512]{0:T(512)(128)(2,1)S(1)} %fusion.33), kind=kOutput, calls=%fused_computation.6 | convolution fusion | flops 3370516480 | bytes 13108224 | tf_op jit(solution)/shard_map/dot_general | solution.py:73
  122.5 79.0 %all-gather.5.cloned.1.call-done = bf16[1,1280,1,2560]{3,1,2,0:T(8,128)(2,1)} async-done(((bf16[1,80,1,2560]{3,1,2,0:T(8,128)(2,1)}), bf16[1,1280,1,2560]{3,1,2,0:T(8,128)(2,1)}) %all-gather.5.cloned.1.call-update) | async-done | bytes 6553616 | tf_op jit(solution)/shard_map/all_gather | solution.py:63
  201.6 7.9 %multiply_convert_fusion.1 = bf16[512,2560]{1,0:T(8,128)(2,1)S(1)} fusion(f32[512,2560]{1,0:T(8,128)} %copy-done.9, bf16[1,1280,1,2560]{3,1,2,0:T(8,128)(2,1)} %all-gather.5.cloned.1.call-done, bf16[1,512,1280]{2,1,0:T(8,128)(2,1)S(1)} %copy-done.6, bf16[512]{0:T(512)(128)(2,1)S(1)} %fusion.33), kind=kOutput, calls=%fused_computation.13 | convolution fusion | flops 3371827200 | bytes 15729664 | tf_op jit(solution)/shard_map/dot_general | solution.py:35
  209.5 0.0 copy-done.5
  209.5 0.0 copy-start.3
  209.5 3.9 fusion.3
  213.4 0.0 copy-done.3
  213.4 5.6 pad_maximum_fusion
  219.0 0.0 reduce-scatter.2.cloned.1.call-update
  219.0 0.2 all-reduce.2.cloned.1.call-start
  219.2 176.1 %reduce-scatter.2.cloned.1.call-done = bf16[80,2,2560]{2,0,1:T(8,128)(2,1)} async-done(((bf16[1280,2,2560]{2,0,1:T(8,128)(2,1)}), bf16[80,2,2560]{2,0,1:T(8,128)(2,1)}) %reduce-scatter.2.cloned.1.call-update) | async-done | bytes 819216 | tf_op jit(solution)/shard_map/reduce_scatter | solution.py:76
  395.3 0.0 copy-done.2
  395.3 5.4 fusion.21
  400.7 0.0 all-reduce.2.cloned.1.call-update
  400.8 2.4 copy.29
  403.2 160.2 %all-reduce.2.cloned.1.call-done = f32[80,2,2560]{2,0,1:T(8,128)} async-done(((f32[80,2,2560]{2,0,1:T(8,128)}), f32[80,2,2560]{2,0,1:T(8,128)}) %all-reduce.2.cloned.1.call-update) | async-done | bytes 1638416 | tf_op jit(solution)/shard_map/psum | solution.py:89
  563.4 0.0 copy-done.4
  563.4 2.8 fusion.27
  566.2 2.4 copy.31
  568.6 2.4 copy.30
  (9 shorter events, 0.0 us)
Async XLA Ops:
  7.2 4.7 copy-start
  7.2 101.2 %all-gather.7.cloned.1.call-start = ((), (), s32[]{:S(2)}) async-start(), calls=%async_computation.4 | async-start | bytes 6963200 | tf_op jit(solution)/shard_map/all_gather | solution.py:61
  10.9 190.6 %all-gather.5.cloned.1.call-start = ((), (), s32[]{:S(2)}) async-start(), calls=%async_computation.3 | async-start | bytes 6963200 | tf_op jit(solution)/shard_map/all_gather | solution.py:63
  11.0 2.6 copy-start.7
  11.8 383.5 %reduce-scatter.2.cloned.1.call-start = ((), (), s32[]{:S(2)}) async-start(), calls=%async_computation.1 | async-start | bytes 13926400 | tf_op jit(solution)/shard_map/reduce_scatter | solution.py:76
  13.6 2.6 copy-start.8
  16.1 2.2 copy-start.1
  20.8 96.0 %copy-start.6 = (bf16[1,512,1280]{2,1,0:T(8,128)(2,1)S(1)}, bf16[1,512,1280]{2,1,0:T(8,128)(2,1)}, u32[]{:S(2)}) copy-start(bf16[1,512,1280]{2,1,0:T(8,128)(2,1)} %param.10) | copy-start | bytes 3932164
  114.4 2.3 copy-start.9
  122.5 87.0 %copy-start.5 = (bf16[512,1280]{1,0:T(8,128)(2,1)S(1)}, bf16[512,1280]{1,0:T(8,128)(2,1)}, u32[]{:S(2)}) copy-start(bf16[512,1280]{1,0:T(8,128)(2,1)} %fusion.16) | copy-start | bytes 3932164
  209.5 3.9 copy-start.3
  219.0 176.4 %copy-start.2 = (bf16[1,80,2,2560]{3,2,1,0:T(2,128)(2,1)S(1)}, bf16[1,80,2,2560]{3,2,1,0:T(2,128)(2,1)}, u32[]{:S(2)}) copy-start(bf16[1,80,2,2560]{3,2,1,0:T(2,128)(2,1)} %param.13) | copy-start | bytes 2457604
  219.0 344.4 %all-reduce.2.cloned.1.call-start = ((), (), s32[]{:S(2)}) async-start(), calls=%async_computation.2 | async-start | bytes 3276800 | tf_op jit(solution)/shard_map/psum | solution.py:89
  400.7 162.7 %copy-start.4 = (f32[80,2,2560]{2,1,0:T(2,128)S(1)}, f32[80,2,2560]{2,1,0:T(2,128)}, u32[]{:S(2)}) copy-start(f32[80,2,2560]{2,1,0:T(2,128)} %param.16) | copy-start | bytes 4915204
Sparse Core Ops, SparseCore 0:
  11.3 97.0 all-gather.6
  111.6 89.9 all-gather.4
  219.1 176.1 reduce-scatter.1
  400.9 162.4 all-reduce.1
where the time goes:
time: 578 us
  waiting for transfers between devices  503 us (87%)
  matrix products  23.7 us (4%)
  other arithmetic  20 us (3%)
  local copies, waits for them, and re-layouts  16.6 us (3%)
  between operations  13.9 us (2%)
    reduce_scatter x1, waiting for transfers between devices, per_device(): lax.psum_scatter(jnp.stack((grad_in, grad_out), axis=1).astype(jnp.bfloat...  176 us
    psum x1, waiting for transfers between devices, per_device(): totals = lax.psum(pseudo, 'group')  160 us
    all_gather x1, waiting for transfers between devices, per_device(): lax.all_gather(inner_params[0, :, 0, :], 'fsdp', axis=0, tiled=True)  87.6 us
    all_gather x1, waiting for transfers between devices, per_device(): lax.all_gather(inner_params[0, :, 1, :], 'fsdp', axis=0, tiled=True)  79 us
    dot_general x2, matrix products, add_rows(): return jnp.dot(left_rows, portion, preferred_element_type=jnp.float32)  14 us
  transfers between devices with their start and end apart: 4, of which 4 were waited for; matrix products, arithmetic and copies ran while one was open for 4% of the time, Pallas kernels for 0%

commit v1 on v0

--- a/solution.py
+++ b/solution.py
@@ -86,7 +86,8 @@
     stepped = current - inner_rate * (update + decay_rate * current)
     pseudo = outer_params - stepped
     replica_count = lax.axis_size("group")
-    totals = lax.psum(pseudo, "group")
+    shards = lax.all_gather(pseudo, "group", axis=0, tiled=False)
+    totals = shards.sum(axis=0)
     average = totals * (1.0 / replica_count)
     new_momentum = nesterov_mu * momentum + average
     new_outer = outer_params - outer_rate * (average + nesterov_mu * new_momentum)

time: 578 us -> 704 us (1.22)
  waiting for transfers between devices: 503 us -> 619 us
  other arithmetic: 20 us -> 29.9 us
    all_gather x0 -> x1, waiting for transfers between devices: none -> 276 us  [per_device(): shards = lax.all_gather(pseudo, 'group', axis=0, tiled=False)]
    psum x1 -> x0, waiting for transfers between devices: 160 us -> none  [per_device(): totals = lax.psum(pseudo, 'group')]
    reduce_sum x0 -> x1, other arithmetic: none -> 10.3 us  [per_device(): totals = shards.sum(axis=0)]
  transfers between devices with their start and end apart: 4 -> 4, of which waited for: 4 -> 4; matrix products, arithmetic and copies ran while one was open for 4% -> 3% of each run, Pallas kernels for 0% -> 0%
where the time goes in v1:
time: 704 us; the launch traced here: 703 us
  waiting for transfers between devices  619 us (88%)
  other arithmetic  29.9 us (4%)
  matrix products  23.7 us (3%)
  local copies, waits for them, and re-layouts  16.6 us (2%)
  between operations  13.9 us (2%)
    all_gather x1, waiting for transfers between devices, per_device(): shards = lax.all_gather(pseudo, 'group', axis=0, tiled=False)  276 us
    reduce_scatter x1, waiting for transfers between devices, per_device(): lax.psum_scatter(jnp.stack((grad_in, grad_out), axis=1).astype(jnp.bfloat...  176 us
    all_gather x1, waiting for transfers between devices, per_device(): lax.all_gather(inner_params[0, :, 0, :], 'fsdp', axis=0, tiled=True)  87.6 us
    all_gather x1, waiting for transfers between devices, per_device(): lax.all_gather(inner_params[0, :, 1, :], 'fsdp', axis=0, tiled=True)  79 us
  transfers between devices with their start and end apart: 4, of which 4 were waited for; matrix products, arithmetic and copies ran while one was open for 3% of the time, Pallas kernels for 0%

profile of v1, /device:TPU:2, one launch (start us, length us, event | category | flops | bytes accessed | tf_op | source)
XLA Modules:
  0.0 703.1 jit_solution(8073243558836537714)
XLA Ops:
  7.2 0.0 copy-start
  7.2 0.0 all-gather.9.cloned.1.call-start
  7.2 2.9 fusion.36
  10.1 0.8 copy.53
  10.9 0.0 all-gather.9.cloned.1.call-update
  10.9 0.0 all-gather.7.cloned.1.call-start
  11.0 0.0 copy-start.7
  11.0 0.8 copy.54
  11.8 0.0 all-gather.7.cloned.1.call-update
  11.8 0.0 reduce-scatter.2.cloned.1.call-start
  11.9 0.0 copy-done
  11.9 1.7 convert.32
  13.6 0.0 copy-done.7
  13.6 0.0 copy-start.8
  13.6 2.5 gather_fusion
  16.1 0.0 copy-start.1
  16.1 0.1 broadcast_bitcast_fusion
  16.2 0.0 copy-done.8
  16.2 0.1 fusion.33
  16.2 2.0 fusion.28
  18.2 0.0 copy-done.1
  18.2 0.8 multiply_reduce_fusion
  19.0 1.7 fusion.16
  20.8 87.6 %all-gather.9.cloned.1.call-done = bf16[1,1280,1,2560]{3,1,2,0:T(8,128)(2,1)} async-done(((bf16[1,80,1,2560]{3,1,2,0:T(8,128)(2,1)}), bf16[1,1280,1,2560]{3,1,2,0:T(8,128)(2,1)}) %all-gather.9.cloned.1.call-update) | async-done | bytes 6553616 | tf_op jit(solution)/shard_map/all_gather | solution.py:61
  108.4 6.1 fusion.4
  114.4 0.0 copy-start.9
  114.4 2.3 copy-done.9
  116.7 0.0 copy-done.6
  116.7 5.8 fusion.2
  122.5 79.0 %all-gather.7.cloned.1.call-done = bf16[1,1280,1,2560]{3,1,2,0:T(8,128)(2,1)} async-done(((bf16[1,80,1,2560]{3,1,2,0:T(8,128)(2,1)}), bf16[1,1280,1,2560]{3,1,2,0:T(8,128)(2,1)}) %all-gather.7.cloned.1.call-update) | async-done | bytes 6553616 | tf_op jit(solution)/shard_map/all_gather | solution.py:63
  201.6 7.9 %multiply_convert_fusion.1 = bf16[512,2560]{1,0:T(8,128)(2,1)S(1)} fusion(f32[512,2560]{1,0:T(8,128)} %copy-done.9, bf16[1,1280,1,2560]{3,1,2,0:T(8,128)(2,1)} %all-gather.7.cloned.1.call-done, bf16[1,512,1280]{2,1,0:T(8,128)(2,1)S(1)} %copy-done.6, bf16[512]{0:T(512)(128)(2,1)S(1)} %fusion.33), kind=kOutput, calls=%fused_computation.13 | convolution fusion | flops 3371827200 | bytes 15729664 | tf_op jit(solution)/shard_map/dot_general | solution.py:35
  209.5 0.0 copy-done.5
  209.5 0.0 copy-start.3
  209.5 3.9 fusion.3
  213.4 0.0 copy-done.3
  213.4 5.6 pad_maximum_fusion
  219.0 0.0 reduce-scatter.2.cloned.1.call-update
  219.0 0.2 all-gather.11.cloned.1.call-start
  219.2 176.1 %reduce-scatter.2.cloned.1.call-done = bf16[80,2,2560]{2,0,1:T(8,128)(2,1)} async-done(((bf16[1280,2,2560]{2,0,1:T(8,128)(2,1)}), bf16[80,2,2560]{2,0,1:T(8,128)(2,1)}) %reduce-scatter.2.cloned.1.call-update) | async-done | bytes 819216 | tf_op jit(solution)/shard_map/reduce_scatter | solution.py:76
  395.3 0.0 copy-done.2
  395.3 5.4 fusion.21
  400.7 0.0 all-gather.11.cloned.1.call-update
  400.8 2.4 copy.32
  403.2 275.9 %all-gather.11.cloned.1.call-done = f32[1280,2,2560]{2,0,1:T(8,128)} async-done(((f32[80,2,2560]{2,0,1:T(8,128)}), f32[1280,2,2560]{2,0,1:T(8,128)}) %all-gather.11.cloned.1.call-update) | async-done | bytes 26214416 | tf_op jit(solution)/shard_map/all_gather | solution.py:89
  679.1 10.3 %reduce_sum.29 = f32[80,2,2560]{2,0,1:T(8,128)S(1)} reduce(f32[16,80,2,2560]{3,1,0,2:T(8,128)} %bitcast.74, f32[]{:T(128)} %constant.29.clone.1), dimensions={0}, to_apply=%region_3.4 | reduce | flops 6144000 | bytes 27852804 | tf_op jit(solution)/shard_map/reduce_sum | solution.py:90
  689.4 2.3 fusion.27
  691.7 2.4 copy.34
  694.1 2.4 copy.33
  (10 shorter events, 0.0 us)
Async XLA Ops:
  7.2 4.7 copy-start
  7.2 101.2 %all-gather.9.cloned.1.call-start = ((), (), s32[]{:S(2)}) async-start(), calls=%async_computation.3 | async-start | bytes 6963200 | tf_op jit(solution)/shard_map/all_gather | solution.py:61
  10.9 190.6 %all-gather.7.cloned.1.call-start = ((), (), s32[]{:S(2)}) async-start(), calls=%async_computation.2 | async-start | bytes 6963200 | tf_op jit(solution)/shard_map/all_gather | solution.py:63
  11.0 2.6 copy-start.7
  11.8 383.5 %reduce-scatter.2.cloned.1.call-start = ((), (), s32[]{:S(2)}) async-start(), calls=%async_computation.1 | async-start | bytes 13926400 | tf_op jit(solution)/shard_map/reduce_scatter | solution.py:76
  13.6 2.6 copy-start.8
  16.1 2.2 copy-start.1
  20.8 96.0 %copy-start.6 = (bf16[1,512,1280]{2,1,0:T(8,128)(2,1)S(1)}, bf16[1,512,1280]{2,1,0:T(8,128)(2,1)}, u32[]{:S(2)}) copy-start(bf16[1,512,1280]{2,1,0:T(8,128)(2,1)} %param.10) | copy-start | bytes 3932164
  114.4 2.3 copy-start.9
  122.5 87.0 %copy-start.5 = (bf16[512,1280]{1,0:T(8,128)(2,1)S(1)}, bf16[512,1280]{1,0:T(8,128)(2,1)}, u32[]{:S(2)}) copy-start(bf16[512,1280]{1,0:T(8,128)(2,1)} %fusion.16) | copy-start | bytes 3932164
  209.5 3.9 copy-start.3
  219.0 176.4 %copy-start.2 = (bf16[1,80,2,2560]{3,2,1,0:T(2,128)(2,1)S(1)}, bf16[1,80,2,2560]{3,2,1,0:T(2,128)(2,1)}, u32[]{:S(2)}) copy-start(bf16[1,80,2,2560]{3,2,1,0:T(2,128)(2,1)} %param.13) | copy-start | bytes 2457604
  219.0 460.0 %all-gather.11.cloned.1.call-start = ((), (), s32[]{:S(2)}) async-start(), calls=%async_computation.4 | async-start | bytes 27852800 | tf_op jit(solution)/shard_map/all_gather | solution.py:89
  679.1 10.3 %copy-start.4 = (f32[80,2,2560]{2,1,0:T(2,128)S(1)}, f32[80,2,2560]{2,1,0:T(2,128)}, u32[]{:S(2)}) copy-start(f32[80,2,2560]{2,1,0:T(2,128)} %param.16) | copy-start | bytes 4915204
Sparse Core Ops, SparseCore 0:
  11.3 97.0 all-gather.8
  111.6 89.9 all-gather.6
  219.1 176.1 reduce-scatter.1
  400.9 278.1 all-gather.10
